TPU v7x, 32 devices: a whole 2x2x4 slice. The times are simulated.
32 devices in a mesh: point: 8 (over y, x, core), batch: 4 (over z).
Axes of the slice: x: 2, y: 2, z: 4, core: 2. Of those that a mesh axis runs over, the one named last changes fastest.
Arguments:
- activations: bfloat16 [128, 14, 14, 1024], P('batch'), may hold values from -8 to 8
- labels: int32 [128], P('batch'), may hold values from 0 to 999
- t_values: float32 [64], replicated, may hold values from 0 to 1
- point_index: int32 [8], replicated, may hold values from 0 to 63
- w_reduce: bfloat16 [3, 1024, 256], P(None, 'point'), may hold values from -1 to 1
- w_spatial: bfloat16 [3, 2304, 256], P(None, 'point'), may hold values from -0.125 to 0.125
- w_expand: bfloat16 [3, 256, 1024], P(None, 'point'), may hold values from -0.375 to 0.375
- w_classes: bfloat16 [3, 1000, 1024], P(None, None, 'point'), may hold values from -0.1875 to 0.1875
- norm_gain: float32 [3, 1536], replicated, may hold values from 0.5 to 1.5
- norm_bias: float32 [3, 1536], replicated, may hold values from -3 to 3
- class_bias: float32 [3, 1000], replicated, may hold values from -3 to 3
Outputs:
- mean_reduce: float32 [8, 256], P('point')
- var_reduce: float32 [8, 256], P('point')
- mean_spatial: float32 [8, 256], P('point')
- var_spatial: float32 [8, 256], P('point')
- mean_expand: float32 [8, 1024], P('point')
- var_expand: float32 [8, 1024], P('point')
- margin: float32 [8], replicated
All inputs are finite; a program needn't handle non-finite values.
Results may differ from a plain program's by a relative error of at most 0.003.
Values may be sent and summed in bfloat16 or wider, within the bound.
A program may use at most 128 MiB of HBM per device.

v0:
```python
import jax
import jax.numpy as jnp
from jax import lax
from jax.sharding import PartitionSpec as P

EPSILON = 1e-05


def curve_coefficients(t_values, point_index):
    table_size = t_values.shape[0]
    matches = point_index[:, None] == jnp.arange(table_size, dtype=jnp.int32)[None, :]
    picked = jnp.sum(jnp.where(matches, t_values[None, :], 0.0), axis=1)
    doubled = 2.0 * picked
    return jnp.stack(
        [
            jnp.maximum(1.0 - doubled, 0.0),
            1.0 - jnp.abs(1.0 - doubled),
            jnp.maximum(doubled - 1.0, 0.0),
        ],
        axis=1,
    )


def blend_all(coefficients, endpoints):
    target_shape = (coefficients.shape[0],) + (1,) * (endpoints.ndim - 1)
    start_part = coefficients[:, 0].reshape(target_shape) * endpoints[0].astype(jnp.float32)[None]
    bend_part = coefficients[:, 1].reshape(target_shape) * endpoints[1].astype(jnp.float32)[None]
    final_part = coefficients[:, 2].reshape(target_shape) * endpoints[2].astype(jnp.float32)[None]
    return start_part + bend_part + final_part


def point_weight(endpoints, own_row, by_columns):
    if by_columns:
        gathered = lax.all_gather(endpoints, "point", axis=2, tiled=True)
    else:
        gathered = lax.all_gather(endpoints, "point", axis=1, tiled=True)
    return blend_all(own_row, gathered)[0].astype(jnp.bfloat16)


def map_product(maps, kernel):
    return lax.dot_general(
        maps, kernel, (((3,), (0,)), ((), ())), preferred_element_type=jnp.float32
    )


def batch_norm(pre_norm, gain_part, bias_part, row_count):
    channel_total, channel_squares = lax.psum(
        (jnp.sum(pre_norm, axis=(0, 1, 2)), jnp.sum(pre_norm * pre_norm, axis=(0, 1, 2))), "batch"
    )
    channel_mean = channel_total / row_count
    channel_var = channel_squares / row_count - channel_mean * channel_mean
    scaled = (pre_norm - channel_mean) * lax.rsqrt(channel_var + EPSILON) * gain_part + bias_part
    return (channel_mean, channel_var, scaled)


def spatial_conv(source, kernel):
    side_len = source.shape[1]
    middle = source.shape[3]
    padded = jnp.pad(source, ((0, 0), (1, 1), (1, 1), (0, 0)))
    widened = jnp.concatenate(
        [
            padded[:, :, 0:side_len, :],
            padded[:, :, 1 : side_len + 1, :],
            padded[:, :, 2 : side_len + 2, :],
        ],
        axis=3,
    )
    summed = map_product(widened[:, 0:side_len], kernel[0 : 3 * middle])
    summed = summed + map_product(widened[:, 1 : side_len + 1], kernel[3 * middle : 6 * middle])
    summed = summed + map_product(widened[:, 2 : side_len + 2], kernel[6 * middle : 9 * middle])
    return summed


def shards(
    activations,
    labels,
    t_values,
    point_index,
    w_reduce,
    w_spatial,
    w_expand,
    w_classes,
    norm_gain,
    norm_bias,
    class_bias,
):
    coefficients = curve_coefficients(t_values, point_index)
    own_row = lax.dynamic_slice_in_dim(coefficients, lax.axis_index("point"), 1, 0)
    reduce_w = point_weight(w_reduce, own_row, False)
    spatial_w = point_weight(w_spatial, own_row, False)
    expand_w = point_weight(w_expand, own_row, False)
    class_w = point_weight(w_classes, own_row, True)
    gain_now = blend_all(own_row, norm_gain)[0]
    bias_now = blend_all(own_row, norm_bias)[0]
    shift_now = blend_all(own_row, class_bias)[0]
    images, side_len, _, channels = activations.shape
    middle = w_reduce.shape[2]
    row_count = float(images * side_len * side_len * lax.axis_size("batch"))
    reduced = map_product(activations, reduce_w)
    mean_one, var_one, normed_one = batch_norm(
        reduced, gain_now[:middle], bias_now[:middle], row_count
    )
    first = jax.nn.relu(normed_one).astype(jnp.bfloat16)
    spatial = spatial_conv(first, spatial_w)
    mean_two, var_two, normed_two = batch_norm(
        spatial, gain_now[middle : 2 * middle], bias_now[middle : 2 * middle], row_count
    )
    second = jax.nn.relu(normed_two).astype(jnp.bfloat16)
    expanded = map_product(second, expand_w)
    mean_three, var_three, normed_three = batch_norm(
        expanded, gain_now[2 * middle :], bias_now[2 * middle :], row_count
    )
    block_out = jax.nn.relu(normed_three + activations.astype(jnp.float32))
    pooled = jnp.mean(block_out, axis=(1, 2)).astype(jnp.bfloat16)
    logits = (
        lax.dot_general(
            pooled, class_w, (((1,), (1,)), ((), ())), preferred_element_type=jnp.float32
        )
        + shift_now
    )
    classes = logits.shape[1]
    onehot = labels[:, None] == jnp.arange(classes, dtype=jnp.int32)[None, :]
    correct = jnp.sum(jnp.where(onehot, logits, 0.0), axis=1)
    rivals = jnp.max(jnp.where(onehot, -1e30, logits), axis=1)
    partial_value = jnp.sum(correct - rivals) / (images * lax.axis_size("batch"))
    point_count = point_index.shape[0]
    placed = jnp.where(
        jnp.arange(point_count, dtype=jnp.int32) == lax.axis_index("point"), partial_value, 0.0
    )
    margin_all = lax.psum(placed, ("point", "batch"))
    return (
        mean_one[None],
        var_one[None],
        mean_two[None],
        var_two[None],
        mean_three[None],
        var_three[None],
        margin_all,
    )


def solution(mesh):
    placed = (
        P("batch", None, None, None),
        P("batch"),
        P(),
        P(),
        P(None, "point", None),
        P(None, "point", None),
        P(None, "point", None),
        P(None, None, "point"),
        P(),
        P(),
        P(),
    )
    return jax.shard_map(
        shards,
        mesh=mesh,
        in_specs=placed,
        out_specs=(
            P("point", None),
            P("point", None),
            P("point", None),
            P("point", None),
            P("point", None),
            P("point", None),
            P(),
        ),
        check_vma=False,
    )
```

profile of v0, /device:TPU:0, one launch (start us, length us, event | category | flops | bytes accessed | tf_op | source)
XLA Modules:
  0.0 208.5 jit_solution(10090536275269189656)
XLA Ops:
  7.2 0.0 all-gather.5.cloned.1.call-start
  7.2 0.7 all-gather.5.cloned.1.call-update
  7.9 0.0 all-gather.7.cloned.1.call-start
  7.9 0.7 all-gather.7.cloned.1.call-update
  8.7 0.0 all-gather.9.cloned.1.call-start
  8.7 0.7 all-gather.9.cloned.1.call-update
  9.4 0.0 all-gather.11.cloned.1.call-start
  9.4 0.5 all-gather.11.cloned.1.call-update
  10.0 0.9 select_reduce_fusion.2
  10.8 0.1 constant_dynamic-slice_fusion
  10.9 0.6 fusion.37
  11.5 2.8 %multiply_add_fusion = (f32[1,1536]{1,0:T(1,128)S(1)}, f32[1,1536]{1,0:T(1,128)S(1)}) fusion(f32[3,1536]{1,0:T(4,128)} %param.20, f32[]{:T(128)} %bitcast.5, f32[]{:T(128)} %bitcast.4, f32[]{:T(128)} %bitcast.3, f32[3,1536]{1,0:T(4,128)} %param.19), kind=kLoop, calls=%fused_computation.50 | loop fusion | flops 15360 | bytes 49164 | tf_op jit(solution)/shard_map/add | solution.py:29
  14.3 2.7 %multiply_add_fusion.2 = f32[1,1000]{1,0:T(1,128)S(1)} fusion(f32[3,1000]{1,0:T(4,128)} %param.21, f32[]{:T(128)} %bitcast.5, f32[]{:T(128)} %bitcast.4, f32[]{:T(128)} %bitcast.3), kind=kLoop, calls=%fused_computation.52 | loop fusion | flops 5000 | bytes 16012 | tf_op jit(solution)/shard_map/add | solution.py:29
  17.0 21.2 %all-gather.5.cloned.1.call-done = bf16[3,1024,256]{2,1,0:T(8,128)(2,1)} async-done(((bf16[3,128,256]{2,1,0:T(8,128)(2,1)}), bf16[3,1024,256]{2,1,0:T(8,128)(2,1)}) %all-gather.5.cloned.1.call-update) | async-done | bytes 1572880 | tf_op jit(solution)/shard_map/all_gather | solution.py:36
  38.2 13.3 %multiply_reduce_fusion.2 = (f32[256]{0:T(256)S(1)}, f32[256]{0:T(256)S(1)}, f32[256,32,14,14]{0,1,3,2:T(8,128)}) fusion(bf16[32,14,14,1024]{3,0,2,1:T(8,128)(2,1)} %param.11, bf16[3,1024,256]{2,1,0:T(8,128)(2,1)} %all-gather.5.cloned.1.call-done, f32[]{:T(128)} %bitcast.5, f32[]{:T(128)} %bitcast.4, f32[]{:T(128)} %bitcast.3), kind=kOutput, calls=%fused_computation.7 | convolution fusion | flops 3295510016 | bytes 20842508 | tf_op jit(solution)/shard_map/dot_general | solution.py:41
  51.5 11.7 %all-reduce.3 = (f32[256]{0:T(256)S(1)}, f32[256]{0:T(256)S(1)}) all-reduce(f32[256]{0:T(256)S(1)} %get-tuple-element.12, f32[256]{0:T(256)S(1)} %get-tuple-element.11), channel_id=1, replica_groups=mesh['point'=8,'batch'=4] {'batch'}, use_global_device_ids=true, to_apply=%region_2.3 | all-reduce | flops 512 | bytes 4096 | tf_op jit(solution)/shard_map/psum | solution.py:47
  63.2 0.6 add_rsqrt_fusion.2
  63.8 0.0 copy-start.4
  63.8 4.1 %fusion.1 = bf16[32,14,14,256]{3,0,2,1:T(8,128)(2,1)S(1)} fusion(f32[256,32,14,14]{0,1,3,2:T(8,128)} %get-tuple-element.43, f32[256]{0:T(256)S(1)} %bitcast.77, f32[256]{0:T(256)S(1)} %bitcast.78, f32[256]{0:T(256)S(1)} %get-tuple-element.25, f32[256]{0:T(256)S(1)} %get-tuple-element.39), kind=kLoop, calls=%fused_computation.13 | loop fusion | flops 9633792 | bytes 9637888 | tf_op jit(solution)/shard_map/convert_element_type | solution.py:103
  67.9 4.9 %pad_slice_fusion.2 = (bf16[32,16,14,256]{3,0,2,1:T(8,128)(2,1)}, bf16[32,16,14,256]{3,0,2,1:T(8,128)(2,1)}, bf16[32,16,14,256]{3,0,2,1:T(8,128)(2,1)}) fusion(bf16[32,14,14,256]{3,0,2,1:T(8,128)(2,1)S(1)} %fusion.1), kind=kLoop, calls=%fused_computation.10 | loop fusion | bytes 14221312 | tf_op jit(solution)/shard_map/slice | solution.py:62
  72.8 0.0 copy-done.4
  72.8 1.2 all-gather.7.cloned.1.call-done
  74.0 4.5 %add_convert_fusion.1 = bf16[1,2304,256]{2,1,0:T(8,128)(2,1)S(1)} fusion(bf16[3,2304,256]{2,1,0:T(8,128)(2,1)} %all-gather.7.cloned.1.call-done, f32[]{:T(128)} %bitcast.5, f32[]{:T(128)} %bitcast.4, f32[]{:T(128)} %bitcast.3), kind=kLoop, calls=%fused_computation.19 | loop fusion | flops 5308416 | bytes 4718604 | tf_op jit(solution)/shard_map/convert_element_type | solution.py:37
  78.5 0.0 copy-start
  78.5 0.0 copy-start.1
  78.5 0.0 copy-start.2
  78.5 7.3 %fusion.31 = f32[32,14,14,256]{3,0,2,1:T(8,128)} fusion(bf16[1,2304,256]{2,1,0:T(8,128)(2,1)S(1)} %add_convert_fusion.1, bf16[32,16,14,256]{3,0,2,1:T(8,128)(2,1)} %get-tuple-element.29, bf16[32,16,14,256]{3,0,2,1:T(8,128)(2,1)} %get-tuple-element.28, bf16[32,16,14,256]{3,0,2,1:T(8,128)(2,1)} %get-tuple-element.27), kind=kOutput, calls=%fused_computation.44 | convolution fusion | flops 2499280896 | bytes 17825792 | tf_op jit(solution)/shard_map/dot_general | solution.py:41
  85.8 0.0 copy-done
  85.8 1.2 copy-done.1
  87.0 1.0 copy-done.2
  88.0 5.4 %fusion.30 = f32[32,14,14,256]{3,0,2,1:T(8,128)} fusion(bf16[1,2304,256]{2,1,0:T(8,128)(2,1)S(1)} %add_convert_fusion.1, bf16[32,16,14,256]{3,0,2,1:T(8,128)(2,1)S(1)} %copy-done.2, bf16[32,16,14,256]{3,0,2,1:T(8,128)(2,1)S(1)} %copy-done.1, bf16[32,16,14,256]{3,0,2,1:T(8,128)(2,1)S(1)} %copy-done), kind=kOutput, calls=%fused_computation.42 | convolution fusion | flops 2499280896 | bytes 17825792 | tf_op jit(solution)/shard_map/dot_general | solution.py:41
  93.4 9.0 %multiply_reduce_fusion.1 = (f32[256]{0:T(256)S(1)}, f32[256]{0:T(256)S(1)}, f32[32,14,14,256]{3,0,2,1:T(8,128)}) fusion(bf16[1,2304,256]{2,1,0:T(8,128)(2,1)S(1)} %add_convert_fusion.1, bf16[32,16,14,256]{3,0,2,1:T(8,128)(2,1)S(1)} %copy-done.2, bf16[32,16,14,256]{3,0,2,1:T(8,128)(2,1)S(1)} %copy-done.1, bf16[32,16,14,256]{3,0,2,1:T(8,128)(2,1)S(1)} %copy-done, ...), kind=kOutput, calls=%fused_computation.5 | convolution fusion | flops 2507308544 | bytes 30672896 | tf_op jit(solution)/shard_map/dot_general | solution.py:41
  102.4 11.9 %all-reduce.2 = (f32[256]{0:T(256)S(1)}, f32[256]{0:T(256)S(1)}) all-reduce(f32[256]{0:T(256)S(1)} %get-tuple-element.10, f32[256]{0:T(256)S(1)} %get-tuple-element.9), channel_id=1, replica_groups=mesh['point'=8,'batch'=4] {'batch'}, use_global_device_ids=true, to_apply=%region_6.7 | all-reduce | flops 512 | bytes 4096 | tf_op jit(solution)/shard_map/psum | solution.py:47
  114.4 0.6 add_rsqrt_fusion.1
  114.9 0.0 copy-start.5
  114.9 0.0 all-gather.9.cloned.1.call-done
  114.9 16.0 %multiply_reduce_fusion = (f32[1024]{0:T(1024)S(1)}, f32[1024]{0:T(1024)S(1)}, f32[32,14,14,1024]{3,0,2,1:T(8,128)}) fusion(bf16[3,256,1024]{2,1,0:T(8,128)(2,1)} %all-gather.9.cloned.1.call-done, f32[]{:T(128)} %bitcast.5, f32[]{:T(128)} %bitcast.4, f32[]{:T(128)} %bitcast.3, f32[32,14,14,256]{3,0,2,1:T(8,128)} %get-tuple-element.44, f32[256]{0:T(256)S(1)} %bitcast.84, ...), kind=kOutput, calls=%fused_computation.1 | convolution fusion | flops 3319592960 | bytes 33697804 | tf_op jit(solution)/shard_map/dot_general | solution.py:41
  130.9 0.0 copy-done.5
  130.9 8.5 %all-reduce.1 = (f32[1024]{0:T(1024)S(1)}, f32[1024]{0:T(1024)S(1)}) all-reduce(f32[1024]{0:T(1024)S(1)} %get-tuple-element.8, f32[1024]{0:T(1024)S(1)} %get-tuple-element.7), channel_id=1, replica_groups=mesh['point'=8,'batch'=4] {'batch'}, use_global_device_ids=true, to_apply=%region_10.11 | all-reduce | flops 2048 | bytes 16384 | tf_op jit(solution)/shard_map/psum | solution.py:47
  139.5 0.6 add_rsqrt_fusion
  140.1 0.0 copy-start.3
  140.1 0.0 copy-start.6
  140.1 14.9 %maximum_reduce_fusion = f32[32,1024]{1,0:T(8,128)S(1)} fusion(bf16[32,14,14,1024]{3,0,2,1:T(8,128)(2,1)} %param.11, f32[32,14,14,1024]{3,0,2,1:T(8,128)} %get-tuple-element.45, f32[1024]{0:T(1024)S(1)} %bitcast.74, f32[1024]{0:T(1024)S(1)} %bitcast.75, f32[1024]{0:T(1024)S(1)} %get-tuple-element.21, f32[1024]{0:T(1024)S(1)} %get-tuple-element.34), kind=kLoop, calls=%fused_computation | loop fusion | flops 51347456 | bytes 38682624 | tf_op jit(solution)/shard_map/reduce_sum | solution.py:114
  154.9 0.0 copy-done.3
  154.9 0.0 all-gather.11.cloned.1.call-done
  155.0 0.0 copy-done.6
  155.0 6.1 %select_reduce_fusion = (f32[32]{0:T(128)S(1)}, f32[32]{0:T(128)S(1)}) fusion(s32[32]{0:T(128)S(1)} %copy-done.6, f32[1000]{0:T(1024)S(1)} %bitcast.80, bf16[3,1000,1024]{2,1,0:T(8,128)(2,1)} %all-gather.11.cloned.1.call-done, f32[]{:T(128)} %bitcast.5, f32[]{:T(128)} %bitcast.4, f32[]{:T(128)} %bitcast.3, f32[32,1024]{1,0:T(8,128)S(1)} %maximum_reduce_fusion), kind=kOutput, calls=%fused_computation.45 | convolution fusion | flops 75009472 | bytes 6279468 | tf_op jit(solution)/shard_map/dot_general | solution.py:116
  161.1 0.6 subtract_reduce_fusion
  162.4 39.6 %psum.55 = f32[8]{0:T(128)} all-reduce(f32[8]{0:T(128)S(1)} %compare_select_fusion), channel_id=1, replica_groups=mesh['point'=8,'batch'=4] {'point','batch'}, use_global_device_ids=true, to_apply=%region_17.18 | all-reduce | flops 8 | bytes 64 | tf_op jit(solution)/shard_map/psum | solution.py:130
  (7 shorter events, 0.0 us)
Async XLA Ops:
  7.2 31.0 %all-gather.5.cloned.1.call-start = ((), (), s32[]{:S(2)}) async-start(), calls=%async_computation | async-start | bytes 1769472 | tf_op jit(solution)/shard_map/all_gather | solution.py:36
  7.9 66.1 %all-gather.7.cloned.1.call-start = ((), (), s32[]{:S(2)}) async-start(), calls=%async_computation.1 | async-start | bytes 3981312 | tf_op jit(solution)/shard_map/all_gather | solution.py:36
  8.7 106.3 %all-gather.9.cloned.1.call-start = ((), (), s32[]{:S(2)}) async-start(), calls=%async_computation.2 | async-start | bytes 1769472 | tf_op jit(solution)/shard_map/all_gather | solution.py:36
  9.4 145.6 %all-gather.11.cloned.1.call-start = ((), (), s32[]{:S(2)}) async-start(), calls=%async_computation.3 | async-start | bytes 6912000 | tf_op jit(solution)/shard_map/all_gather | solution.py:34
  63.8 9.0 %copy-start.4 = (f32[256]{0:T(256)}, f32[256]{0:T(256)S(1)}, u32[]{:S(2)}) copy-start(f32[256]{0:T(256)S(1)} %get-tuple-element.39) | copy-start | bytes 3076
  78.5 7.3 %copy-start = (bf16[32,16,14,256]{3,0,2,1:T(8,128)(2,1)S(1)}, bf16[32,16,14,256]{3,0,2,1:T(8,128)(2,1)}, u32[]{:S(2)}) copy-start(bf16[32,16,14,256]{3,0,2,1:T(8,128)(2,1)} %get-tuple-element.27) | copy-start | bytes 11010052
  78.5 8.5 %copy-start.1 = (bf16[32,16,14,256]{3,0,2,1:T(8,128)(2,1)S(1)}, bf16[32,16,14,256]{3,0,2,1:T(8,128)(2,1)}, u32[]{:S(2)}) copy-start(bf16[32,16,14,256]{3,0,2,1:T(8,128)(2,1)} %get-tuple-element.28) | copy-start | bytes 11010052
  78.5 9.5 %copy-start.2 = (bf16[32,16,14,256]{3,0,2,1:T(8,128)(2,1)S(1)}, bf16[32,16,14,256]{3,0,2,1:T(8,128)(2,1)}, u32[]{:S(2)}) copy-start(bf16[32,16,14,256]{3,0,2,1:T(8,128)(2,1)} %get-tuple-element.29) | copy-start | bytes 11010052
  114.9 16.0 %copy-start.5 = (f32[256]{0:T(256)}, f32[256]{0:T(256)S(1)}, u32[]{:S(2)}) copy-start(f32[256]{0:T(256)S(1)} %get-tuple-element.38) | copy-start | bytes 3076
  140.1 14.9 %copy-start.3 = (f32[1024]{0:T(1024)}, f32[1024]{0:T(1024)S(1)}, u32[]{:S(2)}) copy-start(f32[1024]{0:T(1024)S(1)} %get-tuple-element.34) | copy-start | bytes 12292
  140.1 14.9 %copy-start.6 = (s32[32]{0:T(128)S(1)}, s32[32]{0:T(128)}, u32[]{:S(2)}) copy-start(s32[32]{0:T(128)} %param.12) | copy-start | bytes 388
Sparse Core Ops, SparseCore 0:
  9.9 28.2 all-gather.4
  40.1 33.8 all-gather.6
  75.9 25.5 all-gather.8
  103.2 45.9 all-gather.10
where the time goes:
time: 209 us; the launch traced here: 208 us
  blocking collectives  71.7 us (34%)
  matrix products  57.1 us (27%)
  other arithmetic  32.2 us (15%)
  waiting for transfers between devices  24.9 us (12%)
  between operations  14.6 us (7%)
  local copies, waits for them, and re-layouts  7.82 us (4%)
    dot_general x5, matrix products, map_product(): lax.dot_general(maps, kernel, (((3,), (0,)), ((), ())), preferred_element...  51 us
    psum x1, blocking collectives, shards(): margin_all = lax.psum(placed, ('point', 'batch'))  39.6 us
    psum x3, blocking collectives, batch_norm(): lax.psum((jnp.sum(pre_norm, axis=(0, 1, 2)), jnp.sum(pre_norm * pre_norm,...  32.1 us
    all_gather x3, waiting for transfers between devices, point_weight(): gathered = lax.all_gather(endpoints, 'point', axis=1, tiled=True)  22.3 us
    reduce_sum x1, other arithmetic, shards(): pooled = jnp.mean(block_out, axis=(1, 2)).astype(jnp.bfloat16)  14.9 us
    dot_general x1, matrix products, shards(): lax.dot_general(pooled, class_w, (((1,), (1,)), ((), ())), preferred_elem...  6.09 us
    add x2, other arithmetic, blend_all(): return start_part + bend_part + final_part  5.52 us
    slice x1, local copies, waits for them, and re-layouts, spatial_conv(): padded[:, :, 0:side_len, :]  4.94 us
  transfers between devices with their start and end apart: 4, of which 2 were waited for; matrix products, arithmetic and copies ran while one was open for 42% of the time, Pallas kernels for 0%

commit v1 on v0

--- a/solution.py
+++ b/solution.py
@@ -127,7 +127,7 @@
     placed = jnp.where(
         jnp.arange(point_count, dtype=jnp.int32) == lax.axis_index("point"), partial_value, 0.0
     )
-    margin_all = lax.psum(placed, ("point", "batch"))
+    margin_all = jnp.sum(lax.all_gather(placed, ("point", "batch")), axis=0)
     return (
         mean_one[None],
         var_one[None],

time: 209 us -> 235 us (1.12)
  blocking collectives: 71.7 us -> 97.4 us
    all_gather x0 -> x1, blocking collectives: none -> 65.3 us  [shards(): margin_all = jnp.sum(lax.all_gather(placed, ('point', 'batch')), axis=0)]
    psum x1 -> x0, blocking collectives: 39.6 us -> none  [shards(): margin_all = lax.psum(placed, ('point', 'batch'))]
  transfers between devices with their start and end apart: 4 -> 4, of which waited for: 2 -> 2; matrix products, arithmetic and copies ran while one was open for 42% -> 38% of each run, Pallas kernels for 0% -> 0%
where the time goes in v1:
time: 235 us
  blocking collectives  97.4 us (41%)
  matrix products  57.1 us (24%)
  other arithmetic  32.8 us (14%)
  waiting for transfers between devices  24.9 us (11%)
  between operations  14.6 us (6%)
  local copies, waits for them, and re-layouts  7.82 us (3%)
    all_gather x1, blocking collectives, shards(): margin_all = jnp.sum(lax.all_gather(placed, ('point', 'batch')), axis=0)  65.3 us
    dot_general x5, matrix products, map_product(): lax.dot_general(maps, kernel, (((3,), (0,)), ((), ())), preferred_element...  51 us
    psum x3, blocking collectives, batch_norm(): lax.psum((jnp.sum(pre_norm, axis=(0, 1, 2)), jnp.sum(pre_norm * pre_norm,...  32.1 us
    all_gather x3, waiting for transfers between devices, point_weight(): gathered = lax.all_gather(endpoints, 'point', axis=1, tiled=True)  22.3 us
    reduce_sum x1, other arithmetic, shards(): pooled = jnp.mean(block_out, axis=(1, 2)).astype(jnp.bfloat16)  14.9 us
    dot_general x1, matrix products, shards(): lax.dot_general(pooled, class_w, (((1,), (1,)), ((), ())), preferred_elem...  6.09 us
    add x2, other arithmetic, blend_all(): return start_part + bend_part + final_part  5.52 us
    slice x1, local copies, waits for them, and re-layouts, spatial_conv(): padded[:, :, 0:side_len, :]  4.94 us
  transfers between devices with their start and end apart: 4, of which 2 were waited for; matrix products, arithmetic and copies ran while one was open for 38% of the time, Pallas kernels for 0%

profile of v1, /device:TPU:0, one launch (start us, length us, event | category | flops | bytes accessed | tf_op | source)
XLA Modules:
  0.0 234.8 jit_solution(11276874742730836106)
XLA Ops:
  7.2 0.0 all-gather.6.cloned.1.call-start
  7.2 0.7 all-gather.6.cloned.1.call-update
  7.9 0.0 all-gather.8.cloned.1.call-start
  7.9 0.7 all-gather.8.cloned.1.call-update
  8.7 0.0 all-gather.10.cloned.1.call-start
  8.7 0.7 all-gather.10.cloned.1.call-update
  9.4 0.0 all-gather.12.cloned.1.call-start
  9.4 0.5 all-gather.12.cloned.1.call-update
  10.0 0.9 select_reduce_fusion.2
  10.8 0.1 constant_dynamic-slice_fusion
  10.9 0.6 fusion.38
  11.5 2.8 %multiply_add_fusion = (f32[1,1536]{1,0:T(1,128)S(1)}, f32[1,1536]{1,0:T(1,128)S(1)}) fusion(f32[3,1536]{1,0:T(4,128)} %param.20, f32[]{:T(128)} %bitcast.5, f32[]{:T(128)} %bitcast.4, f32[]{:T(128)} %bitcast.3, f32[3,1536]{1,0:T(4,128)} %param.19), kind=kLoop, calls=%fused_computation.50 | loop fusion | flops 15360 | bytes 49164 | tf_op jit(solution)/shard_map/add | solution.py:29
  14.3 2.7 %multiply_add_fusion.2 = f32[1,1000]{1,0:T(1,128)S(1)} fusion(f32[3,1000]{1,0:T(4,128)} %param.21, f32[]{:T(128)} %bitcast.5, f32[]{:T(128)} %bitcast.4, f32[]{:T(128)} %bitcast.3), kind=kLoop, calls=%fused_computation.52 | loop fusion | flops 5000 | bytes 16012 | tf_op jit(solution)/shard_map/add | solution.py:29
  17.0 21.2 %all-gather.6.cloned.1.call-done = bf16[3,1024,256]{2,1,0:T(8,128)(2,1)} async-done(((bf16[3,128,256]{2,1,0:T(8,128)(2,1)}), bf16[3,1024,256]{2,1,0:T(8,128)(2,1)}) %all-gather.6.cloned.1.call-update) | async-done | bytes 1572880 | tf_op jit(solution)/shard_map/all_gather | solution.py:36
  38.2 13.3 %multiply_reduce_fusion.2 = (f32[256]{0:T(256)S(1)}, f32[256]{0:T(256)S(1)}, f32[256,32,14,14]{0,1,3,2:T(8,128)}) fusion(bf16[32,14,14,1024]{3,0,2,1:T(8,128)(2,1)} %param.11, bf16[3,1024,256]{2,1,0:T(8,128)(2,1)} %all-gather.6.cloned.1.call-done, f32[]{:T(128)} %bitcast.5, f32[]{:T(128)} %bitcast.4, f32[]{:T(128)} %bitcast.3), kind=kOutput, calls=%fused_computation.7 | convolution fusion | flops 3295510016 | bytes 20842508 | tf_op jit(solution)/shard_map/dot_general | solution.py:41
  51.5 11.7 %all-reduce.3 = (f32[256]{0:T(256)S(1)}, f32[256]{0:T(256)S(1)}) all-reduce(f32[256]{0:T(256)S(1)} %get-tuple-element.12, f32[256]{0:T(256)S(1)} %get-tuple-element.11), channel_id=1, replica_groups=mesh['point'=8,'batch'=4] {'batch'}, use_global_device_ids=true, to_apply=%region_2.3 | all-reduce | flops 512 | bytes 4096 | tf_op jit(solution)/shard_map/psum | solution.py:47
  63.2 0.6 add_rsqrt_fusion.2
  63.8 0.0 copy-start.4
  63.8 4.1 %fusion.1 = bf16[32,14,14,256]{3,0,2,1:T(8,128)(2,1)S(1)} fusion(f32[256,32,14,14]{0,1,3,2:T(8,128)} %get-tuple-element.43, f32[256]{0:T(256)S(1)} %bitcast.79, f32[256]{0:T(256)S(1)} %bitcast.80, f32[256]{0:T(256)S(1)} %get-tuple-element.25, f32[256]{0:T(256)S(1)} %get-tuple-element.39), kind=kLoop, calls=%fused_computation.13 | loop fusion | flops 9633792 | bytes 9637888 | tf_op jit(solution)/shard_map/convert_element_type | solution.py:103
  67.9 4.9 %pad_slice_fusion.2 = (bf16[32,16,14,256]{3,0,2,1:T(8,128)(2,1)}, bf16[32,16,14,256]{3,0,2,1:T(8,128)(2,1)}, bf16[32,16,14,256]{3,0,2,1:T(8,128)(2,1)}) fusion(bf16[32,14,14,256]{3,0,2,1:T(8,128)(2,1)S(1)} %fusion.1), kind=kLoop, calls=%fused_computation.10 | loop fusion | bytes 14221312 | tf_op jit(solution)/shard_map/slice | solution.py:62
  72.8 0.0 copy-done.4
  72.8 1.2 all-gather.8.cloned.1.call-done
  74.0 4.5 %add_convert_fusion.1 = bf16[1,2304,256]{2,1,0:T(8,128)(2,1)S(1)} fusion(bf16[3,2304,256]{2,1,0:T(8,128)(2,1)} %all-gather.8.cloned.1.call-done, f32[]{:T(128)} %bitcast.5, f32[]{:T(128)} %bitcast.4, f32[]{:T(128)} %bitcast.3), kind=kLoop, calls=%fused_computation.19 | loop fusion | flops 5308416 | bytes 4718604 | tf_op jit(solution)/shard_map/convert_element_type | solution.py:37
  78.5 0.0 copy-start
  78.5 0.0 copy-start.1
  78.5 0.0 copy-start.2
  78.5 7.3 %fusion.31 = f32[32,14,14,256]{3,0,2,1:T(8,128)} fusion(bf16[1,2304,256]{2,1,0:T(8,128)(2,1)S(1)} %add_convert_fusion.1, bf16[32,16,14,256]{3,0,2,1:T(8,128)(2,1)} %get-tuple-element.29, bf16[32,16,14,256]{3,0,2,1:T(8,128)(2,1)} %get-tuple-element.28, bf16[32,16,14,256]{3,0,2,1:T(8,128)(2,1)} %get-tuple-element.27), kind=kOutput, calls=%fused_computation.44 | convolution fusion | flops 2499280896 | bytes 17825792 | tf_op jit(solution)/shard_map/dot_general | solution.py:41
  85.8 0.0 copy-done
  85.8 1.2 copy-done.1
  87.0 1.0 copy-done.2
  88.0 5.4 %fusion.30 = f32[32,14,14,256]{3,0,2,1:T(8,128)} fusion(bf16[1,2304,256]{2,1,0:T(8,128)(2,1)S(1)} %add_convert_fusion.1, bf16[32,16,14,256]{3,0,2,1:T(8,128)(2,1)S(1)} %copy-done.2, bf16[32,16,14,256]{3,0,2,1:T(8,128)(2,1)S(1)} %copy-done.1, bf16[32,16,14,256]{3,0,2,1:T(8,128)(2,1)S(1)} %copy-done), kind=kOutput, calls=%fused_computation.42 | convolution fusion | flops 2499280896 | bytes 17825792 | tf_op jit(solution)/shard_map/dot_general | solution.py:41
  93.4 9.0 %multiply_reduce_fusion.1 = (f32[256]{0:T(256)S(1)}, f32[256]{0:T(256)S(1)}, f32[32,14,14,256]{3,0,2,1:T(8,128)}) fusion(bf16[1,2304,256]{2,1,0:T(8,128)(2,1)S(1)} %add_convert_fusion.1, bf16[32,16,14,256]{3,0,2,1:T(8,128)(2,1)S(1)} %copy-done.2, bf16[32,16,14,256]{3,0,2,1:T(8,128)(2,1)S(1)} %copy-done.1, bf16[32,16,14,256]{3,0,2,1:T(8,128)(2,1)S(1)} %copy-done, ...), kind=kOutput, calls=%fused_computation.5 | convolution fusion | flops 2507308544 | bytes 30672896 | tf_op jit(solution)/shard_map/dot_general | solution.py:41
  102.4 11.9 %all-reduce.2 = (f32[256]{0:T(256)S(1)}, f32[256]{0:T(256)S(1)}) all-reduce(f32[256]{0:T(256)S(1)} %get-tuple-element.10, f32[256]{0:T(256)S(1)} %get-tuple-element.9), channel_id=1, replica_groups=mesh['point'=8,'batch'=4] {'batch'}, use_global_device_ids=true, to_apply=%region_6.7 | all-reduce | flops 512 | bytes 4096 | tf_op jit(solution)/shard_map/psum | solution.py:47
  114.4 0.6 add_rsqrt_fusion.1
  114.9 0.0 copy-start.5
  114.9 0.0 all-gather.10.cloned.1.call-done
  114.9 16.0 %multiply_reduce_fusion = (f32[1024]{0:T(1024)S(1)}, f32[1024]{0:T(1024)S(1)}, f32[32,14,14,1024]{3,0,2,1:T(8,128)}) fusion(bf16[3,256,1024]{2,1,0:T(8,128)(2,1)} %all-gather.10.cloned.1.call-done, f32[]{:T(128)} %bitcast.5, f32[]{:T(128)} %bitcast.4, f32[]{:T(128)} %bitcast.3, f32[32,14,14,256]{3,0,2,1:T(8,128)} %get-tuple-element.44, f32[256]{0:T(256)S(1)} %bitcast.86, ...), kind=kOutput, calls=%fused_computation.1 | convolution fusion | flops 3319592960 | bytes 33697804 | tf_op jit(solution)/shard_map/dot_general | solution.py:41
  130.9 0.0 copy-done.5
  130.9 8.5 %all-reduce.1 = (f32[1024]{0:T(1024)S(1)}, f32[1024]{0:T(1024)S(1)}) all-reduce(f32[1024]{0:T(1024)S(1)} %get-tuple-element.8, f32[1024]{0:T(1024)S(1)} %get-tuple-element.7), channel_id=1, replica_groups=mesh['point'=8,'batch'=4] {'batch'}, use_global_device_ids=true, to_apply=%region_10.11 | all-reduce | flops 2048 | bytes 16384 | tf_op jit(solution)/shard_map/psum | solution.py:47
  139.5 0.6 add_rsqrt_fusion
  140.1 0.0 copy-start.3
  140.1 0.0 copy-start.6
  140.1 14.9 %maximum_reduce_fusion = f32[32,1024]{1,0:T(8,128)S(1)} fusion(bf16[32,14,14,1024]{3,0,2,1:T(8,128)(2,1)} %param.11, f32[32,14,14,1024]{3,0,2,1:T(8,128)} %get-tuple-element.45, f32[1024]{0:T(1024)S(1)} %bitcast.76, f32[1024]{0:T(1024)S(1)} %bitcast.77, f32[1024]{0:T(1024)S(1)} %get-tuple-element.21, f32[1024]{0:T(1024)S(1)} %get-tuple-element.34), kind=kLoop, calls=%fused_computation | loop fusion | flops 51347456 | bytes 38682624 | tf_op jit(solution)/shard_map/reduce_sum | solution.py:114
  154.9 0.0 copy-done.3
  154.9 0.0 all-gather.12.cloned.1.call-done
  155.0 0.0 copy-done.6
  155.0 6.1 %select_reduce_fusion = (f32[32]{0:T(128)S(1)}, f32[32]{0:T(128)S(1)}) fusion(s32[32]{0:T(128)S(1)} %copy-done.6, f32[1000]{0:T(1024)S(1)} %bitcast.82, bf16[3,1000,1024]{2,1,0:T(8,128)(2,1)} %all-gather.12.cloned.1.call-done, f32[]{:T(128)} %bitcast.5, f32[]{:T(128)} %bitcast.4, f32[]{:T(128)} %bitcast.3, f32[32,1024]{1,0:T(8,128)S(1)} %maximum_reduce_fusion), kind=kOutput, calls=%fused_computation.45 | convolution fusion | flops 75009472 | bytes 6279468 | tf_op jit(solution)/shard_map/dot_general | solution.py:116
  161.1 0.6 subtract_reduce_fusion
  162.4 65.3 %all-gather = f32[32,1,8]{2,1,0:T(1,128)S(1)} all-gather(f32[1,1,8]{2,1,0:T(1,128)S(1)} %fusion.33), channel_id=1, replica_groups=mesh['point'=8,'batch'=4] {'point','batch'}, dimensions={0}, use_global_device_ids=true | all-gather | bytes 1056 | tf_op jit(solution)/shard_map/all_gather | solution.py:130
  227.7 0.6 reduce_sum.109
  (7 shorter events, 0.0 us)
Async XLA Ops:
  7.2 31.0 %all-gather.6.cloned.1.call-start = ((), (), s32[]{:S(2)}) async-start(), calls=%async_computation | async-start | bytes 1769472 | tf_op jit(solution)/shard_map/all_gather | solution.py:36
  7.9 66.1 %all-gather.8.cloned.1.call-start = ((), (), s32[]{:S(2)}) async-start(), calls=%async_computation.1 | async-start | bytes 3981312 | tf_op jit(solution)/shard_map/all_gather | solution.py:36
  8.7 106.3 %all-gather.10.cloned.1.call-start = ((), (), s32[]{:S(2)}) async-start(), calls=%async_computation.2 | async-start | bytes 1769472 | tf_op jit(solution)/shard_map/all_gather | solution.py:36
  9.4 145.6 %all-gather.12.cloned.1.call-start = ((), (), s32[]{:S(2)}) async-start(), calls=%async_computation.3 | async-start | bytes 6912000 | tf_op jit(solution)/shard_map/all_gather | solution.py:34
  63.8 9.0 %copy-start.4 = (f32[256]{0:T(256)}, f32[256]{0:T(256)S(1)}, u32[]{:S(2)}) copy-start(f32[256]{0:T(256)S(1)} %get-tuple-element.39) | copy-start | bytes 3076
  78.5 7.3 %copy-start = (bf16[32,16,14,256]{3,0,2,1:T(8,128)(2,1)S(1)}, bf16[32,16,14,256]{3,0,2,1:T(8,128)(2,1)}, u32[]{:S(2)}) copy-start(bf16[32,16,14,256]{3,0,2,1:T(8,128)(2,1)} %get-tuple-element.27) | copy-start | bytes 11010052
  78.5 8.5 %copy-start.1 = (bf16[32,16,14,256]{3,0,2,1:T(8,128)(2,1)S(1)}, bf16[32,16,14,256]{3,0,2,1:T(8,128)(2,1)}, u32[]{:S(2)}) copy-start(bf16[32,16,14,256]{3,0,2,1:T(8,128)(2,1)} %get-tuple-element.28) | copy-start | bytes 11010052
  78.5 9.5 %copy-start.2 = (bf16[32,16,14,256]{3,0,2,1:T(8,128)(2,1)S(1)}, bf16[32,16,14,256]{3,0,2,1:T(8,128)(2,1)}, u32[]{:S(2)}) copy-start(bf16[32,16,14,256]{3,0,2,1:T(8,128)(2,1)} %get-tuple-element.29) | copy-start | bytes 11010052
  114.9 16.0 %copy-start.5 = (f32[256]{0:T(256)}, f32[256]{0:T(256)S(1)}, u32[]{:S(2)}) copy-start(f32[256]{0:T(256)S(1)} %get-tuple-element.38) | copy-start | bytes 3076
  140.1 14.9 %copy-start.3 = (f32[1024]{0:T(1024)}, f32[1024]{0:T(1024)S(1)}, u32[]{:S(2)}) copy-start(f32[1024]{0:T(1024)S(1)} %get-tuple-element.34) | copy-start | bytes 12292
  140.1 14.9 %copy-start.6 = (s32[32]{0:T(128)S(1)}, s32[32]{0:T(128)}, u32[]{:S(2)}) copy-start(s32[32]{0:T(128)} %param.12) | copy-start | bytes 388
Sparse Core Ops, SparseCore 0:
  9.9 28.2 all-gather.5
  40.1 33.8 all-gather.7
  75.9 25.5 all-gather.9
  103.2 45.9 all-gather.11
